TPU v7x, 512 devices: a whole 4x8x8 slice. The times are simulated.
512 devices in a mesh: row: 16 (over z, y_lo), col: 4 (over x), seq: 8 (over y_hi, core).
Axes of the slice: x: 4, y: 8 (y_hi: 4, y_lo: 2; y = y_hi * 2 + y_lo), z: 8, core: 2. Of those that a mesh axis runs over, the one named last changes fastest.
Arguments:
- pair: bfloat16 [1024, 1024, 128], P(('row', 'seq'), 'col'), may hold values from -6 to 6
- alignment: bfloat16 [128, 1024, 256], P(('row', 'seq'), 'col'), may hold values from -6 to 6
- opm_left: bfloat16 [256, 32], replicated, may hold values from -0.375 to 0.375
- opm_right: bfloat16 [256, 32], replicated, may hold values from -0.375 to 0.375
- opm_out: bfloat16 [1024, 128], replicated, may hold values from -2 to 2
- tri_left: bfloat16 [128, 128], replicated, may hold values from -0.5 to 0.5
- tri_left_gate: bfloat16 [128, 128], replicated, may hold values from -0.5 to 0.5
- tri_right: bfloat16 [128, 128], replicated, may hold values from -0.5 to 0.5
- tri_right_gate: bfloat16 [128, 128], replicated, may hold values from -0.5 to 0.5
- tri_gate: bfloat16 [128, 128], replicated, may hold values from -0.5 to 0.5
- tri_out: bfloat16 [128, 128], replicated, may hold values from -0.5 to 0.5
Outputs:
- pair_out: bfloat16 [1024, 1024, 128], P(('row', 'seq'), 'col')
All inputs are finite; a program needn't handle non-finite values.
Results may differ from a plain program's by a relative error of at most 0.0075.
Values may be sent and summed in bfloat16 or wider, within the bound.
A program may use at most 64 MiB of HBM per device.

v0:
```python
import jax
import jax.numpy as jnp
from jax import lax
from jax.sharding import PartitionSpec as P

EPS = 1e-05


def spread_2(shard, axis, root):
    mine = lax.axis_index(axis) == root
    return lax.psum(jnp.where(mine, shard, jnp.zeros_like(shard)), axis)


def layer_norm(values, axis):
    values = values.astype(jnp.float32)
    center = values - jnp.mean(values, axis=axis, keepdims=True)
    spread = jnp.mean(center * center, axis=axis, keepdims=True)
    return center * lax.rsqrt(spread + EPS)


def contract(local_rows, piece):
    return jnp.einsum("cik,cjk->cij", local_rows, piece, preferred_element_type=jnp.float32)


def on_device(
    pair,
    alignment,
    opm_left,
    opm_right,
    opm_out,
    tri_left,
    tri_left_gate,
    tri_right,
    tri_right_gate,
    tri_gate,
    tri_out,
):
    rows_here, cols_here, pair_width = pair.shape
    seq_here = alignment.shape[0]
    model_width = alignment.shape[2]
    factor_width = opm_left.shape[1]
    hidden = tri_left.shape[1]
    n_row = lax.axis_size("row")
    n_col = lax.axis_size("col")
    n_seq = lax.axis_size("seq")
    seq_normed = (
        layer_norm(alignment, 2).astype(jnp.bfloat16).reshape(seq_here * cols_here, model_width)
    )
    left_proj = (
        jnp.dot(seq_normed, opm_left, preferred_element_type=jnp.float32)
        .astype(jnp.bfloat16)
        .reshape(seq_here, cols_here * factor_width)
    )
    right_proj = (
        jnp.dot(seq_normed, opm_right, preferred_element_type=jnp.float32)
        .astype(jnp.bfloat16)
        .reshape(seq_here, cols_here * factor_width)
    )
    per_col = n_row // n_col
    index_row = lax.axis_index("row")
    root_col = index_row // per_col
    left_all, right_all = (
        lax.all_gather(left_proj, ("row", "seq"), axis=0, tiled=True),
        lax.all_gather(right_proj, ("row", "seq"), axis=0, tiled=True),
    )
    index_seq = lax.axis_index("seq")
    offset = (index_row % per_col * n_seq + index_seq) * (rows_here * factor_width)
    row_slice = lax.dynamic_slice_in_dim(left_all, offset, rows_here * factor_width, 1)
    seqs_all = right_all.shape[0]
    row_factors = spread_2(row_slice, "col", root_col)
    right_wide = right_all.reshape(seqs_all, cols_here, factor_width)
    row_stack = jnp.swapaxes(row_factors.reshape(seqs_all, rows_here, factor_width), 0, 1)

    def outer_row(packed):
        row_vals, pair_row = packed
        outer_sum = jnp.einsum(
            "np,njq->jpq", row_vals, right_wide, preferred_element_type=jnp.float32
        )
        mean_outer = (
            (outer_sum * (1.0 / seqs_all))
            .astype(jnp.bfloat16)
            .reshape(cols_here, factor_width * factor_width)
        )
        return (
            pair_row.astype(jnp.float32)
            + jnp.dot(mean_outer, opm_out, preferred_element_type=jnp.float32)
        ).astype(jnp.bfloat16)

    pair_mid = lax.map(outer_row, (row_stack, pair))
    normed_pair = layer_norm(pair_mid, 2).astype(jnp.bfloat16)
    flat_pair = normed_pair.reshape(rows_here * cols_here, pair_width)

    def project(weight):
        return lax.dot_general(
            weight, flat_pair, (((0,), (1,)), ((), ())), preferred_element_type=jnp.float32
        )

    def gated(weight_gate, weight_value):
        gate_part = jax.nn.sigmoid(project(weight_gate))
        return (
            (gate_part * project(weight_value))
            .astype(jnp.bfloat16)
            .reshape(hidden, rows_here, cols_here)
        )

    left_first = gated(tri_left_gate, tri_left)
    right_first = gated(tri_right_gate, tri_right)
    left_local, right_local = (
        lax.all_to_all(
            lax.all_to_all(left_first, "col", split_axis=0, concat_axis=2, tiled=True),
            "seq",
            split_axis=0,
            concat_axis=1,
            tiled=True,
        ),
        lax.all_to_all(
            lax.all_to_all(right_first, "col", split_axis=0, concat_axis=2, tiled=True),
            "seq",
            split_axis=0,
            concat_axis=1,
            tiled=True,
        ),
    )
    product = contract(left_local, lax.all_gather(right_local, "row", axis=1, tiled=True))
    product = product.astype(jnp.bfloat16)
    returned = lax.all_to_all(
        lax.all_to_all(product, "col", split_axis=2, concat_axis=0, tiled=True),
        "seq",
        split_axis=1,
        concat_axis=0,
        tiled=True,
    )
    per_group = hidden // (n_col * n_seq)
    weights_order = (
        tri_out.reshape(n_col, n_seq, per_group, pair_width)
        .transpose(1, 0, 2, 3)
        .reshape(hidden, pair_width)
    )
    normed_product = layer_norm(returned, 0).astype(jnp.bfloat16)
    update = jnp.einsum(
        "cij,cd->ijd", normed_product, weights_order, preferred_element_type=jnp.float32
    )
    gate_part = jax.nn.sigmoid(
        jnp.dot(flat_pair, tri_gate, preferred_element_type=jnp.float32)
    ).reshape(rows_here, cols_here, pair_width)
    return (pair_mid.astype(jnp.float32) + gate_part * update).astype(jnp.bfloat16)


def solution(mesh):
    return jax.shard_map(
        on_device,
        mesh=mesh,
        in_specs=(
            P(("row", "seq"), "col", None),
            P(("row", "seq"), "col", None),
            P(),
            P(),
            P(),
            P(),
            P(),
            P(),
            P(),
            P(),
            P(),
        ),
        out_specs=P(("row", "seq"), "col", None),
        check_vma=False,
    )
```

profile of v0, /device:TPU:8, one launch (start us, length us, event | category | flops | bytes accessed | tf_op | source)
XLA Modules:
  0.0 817.1 jit_solution(16406924209503788000)
XLA Ops:
  8.7 1.2 convolution_convert_fusion.2
  12.9 222.3 %all-gather.8.cloned.1.call-done = bf16[128,1,8192]{2,1,0:T(2,128)(2,1)} async-done(((bf16[1,1,8192]{2,1,0:T(2,128)(2,1)}), bf16[128,1,8192]{2,1,0:T(2,128)(2,1)}) %all-gather.8.cloned.1.call-update) | async-done | bytes 2097168 | tf_op jit(solution)/shard_map/all_gather | solution.py:63
  237.1 218.4 %all-gather.10.cloned.1.call-done = bf16[128,1,8192]{2,1,0:T(2,128)(2,1)} async-done(((bf16[1,1,8192]{2,1,0:T(2,128)(2,1)}), bf16[128,1,8192]{2,1,0:T(2,128)(2,1)}) %all-gather.10.cloned.1.call-update) | async-done | bytes 2097168 | tf_op jit(solution)/shard_map/all_gather | solution.py:64
  455.5 9.1 %copy.67 = bf16[128,1,8192]{0,2,1:T(8,128)(2,1)} copy(bf16[128,1,8192]{2,1,0:T(2,128)(2,1)} %all-gather.10.cloned.1.call-done) | data formatting | bytes 4194304 | tf_op jit(solution)/shard_map/all_gather | solution.py:64
  464.7 3.0 copy.68
  467.7 40.3 %all-reduce.2.cloned.1.call-done = bf16[8,128,32]{1,2,0:T(8,128)(2,1)} async-done(((bf16[8,128,32]{1,2,0:T(8,128)(2,1)}), bf16[8,128,32]{1,2,0:T(8,128)(2,1)}) %all-reduce.2.cloned.1.call-update) | async-done | bytes 65552 | tf_op jit(solution)/shard_map/psum | solution.py:11
  508.0 21.1 %while.10 = (s32[]{:T(128)}, bf16[8,256,128]{2,1,0:T(8,128)(2,1)S(1)}, bf16[8,256,128]{2,1,0:T(8,128)(2,1)}, bf16[8,128,32]{1,2,0:T(8,128)(2,1)}, bf16[128,256,3...) while((s32[]{:T(128)}, bf16[8,256,128]{2,1,0:T(8,128)(2,1)S(1)}, ...), condition=%wide.region_4.5_spmd, body=%wide.region_3.4_spmd.sunk | while | flops 134840320 | bytes 4596305 | solution.py:89
  509.4 1.2 fusion.68
  512.1 1.2 fusion.68
  514.7 1.2 fusion.68
  517.4 1.2 fusion.68
  520.0 1.2 fusion.68
  522.7 1.2 fusion.68
  525.3 1.2 fusion.68
  528.0 1.2 fusion.68
  531.8 11.3 %all_to_all.99 = bf16[128,8,256]{2,1,0:T(8,128)(2,1)S(1)} all-to-all(bf16[128,8,256]{2,1,0:T(8,128)(2,1)S(1)} %copy.72), channel_id=1, replica_groups=mesh['row'=16,'col'=4,'seq'=8] {'col'}, dimensions={0} | all-to-all | bytes 1048576 | tf_op jit(solution)/shard_map/all_to_all | solution.py:117
  543.2 24.0 %all_to_all.100 = bf16[32,8,1024]{2,1,0:T(8,128)(2,1)S(1)} all-to-all(bf16[32,8,1024]{2,1,0:T(8,128)(2,1)S(1)} %bitcast.131), channel_id=1, replica_groups=mesh['row'=16,'col'=4,'seq'=8] {'seq'}, dimensions={0} | all-to-all | bytes 1048576 | tf_op jit(solution)/shard_map/all_to_all | solution.py:116
  569.1 10.5 %all_to_all.101 = bf16[128,8,256]{2,1,0:T(8,128)(2,1)S(1)} all-to-all(bf16[128,8,256]{2,1,0:T(8,128)(2,1)S(1)} %copy.69), channel_id=1, replica_groups=mesh['row'=16,'col'=4,'seq'=8] {'col'}, dimensions={0} | all-to-all | bytes 1048576 | tf_op jit(solution)/shard_map/all_to_all | solution.py:110
  579.7 26.7 %all_to_all.102 = bf16[32,8,1024]{2,1,0:T(8,128)(2,1)S(1)} all-to-all(bf16[32,8,1024]{2,1,0:T(8,128)(2,1)S(1)} %bitcast.134), channel_id=1, replica_groups=mesh['row'=16,'col'=4,'seq'=8] {'seq'}, dimensions={0} | all-to-all | bytes 1048576 | tf_op jit(solution)/shard_map/all_to_all | solution.py:109
  606.4 153.9 %all-gather.6.cloned.1.call-done = bf16[4,1024,1024]{2,1,0:T(8,128)(2,1)} async-done(((bf16[4,64,1024]{2,1,0:T(8,128)(2,1)}), bf16[4,1024,1024]{2,1,0:T(8,128)(2,1)}) %all-gather.6.cloned.1.call-update) | async-done | bytes 8388624 | tf_op jit(solution)/shard_map/all_gather | solution.py:124
  760.3 6.0 convolution_convert_fusion
  767.9 13.4 %all_to_all.103 = bf16[4,2,32768]{2,1,0:T(2,128)(2,1)S(1)} all-to-all(bf16[4,2,32768]{2,1,0:T(2,128)(2,1)S(1)} %reshape.114), channel_id=1, replica_groups=mesh['row'=16,'col'=4,'seq'=8] {'col'}, dimensions={0} | all-to-all | bytes 1048576 | tf_op jit(solution)/shard_map/all_to_all | solution.py:127
  783.6 6.7 all-to-all-start.5
  790.8 17.9 %all-to-all-done.5 = bf16[16,64,256]{2,0,1:T(8,128)(2,1)S(1)} async-done(((bf16[16,64,256]{2,0,1:T(8,128)(2,1)}), bf16[16,64,256]{2,0,1:T(8,128)(2,1)S(1)}, u32[]{:S(2)}, u32[]{:S(2)}) %all-to-all-start.5) | async-done | bytes 524320 | tf_op jit(solution)/shard_map/all_to_all | solution.py:126
  (79 shorter events, 29.0 us)
Async XLA Ops:
  6.5 524.1 %copy-start = (bf16[128,128]{1,0:T(8,128)(2,1)S(1)}, bf16[128,128]{1,0:T(8,128)(2,1)}, u32[]{:S(2)}) copy-start(bf16[128,128]{1,0:T(8,128)(2,1)} %param.21) | copy-start | bytes 98308
  6.5 228.7 %all-gather.8.cloned.1.call-start = ((), (), s32[]{:S(2)}) async-start(), calls=%async_computation.8 | async-start | bytes 4227072 | tf_op jit(solution)/shard_map/all_gather | solution.py:63
  10.7 444.8 %all-gather.10.cloned.1.call-start = ((), (), s32[]{:S(2)}) async-start(), calls=%async_computation.9 | async-start | bytes 4227072 | tf_op jit(solution)/shard_map/all_gather | solution.py:64
  12.8 495.2 %all-reduce.2.cloned.1.call-start = ((), (), s32[]{:S(2)}) async-start(), calls=%async_computation.6 | async-start | bytes 131072 | tf_op jit(solution)/shard_map/psum | solution.py:11
  237.1 523.2 %all-gather.6.cloned.1.call-start = ((), (), s32[]{:S(2)}) async-start(), calls=%async_computation.7 | async-start | bytes 8912896 | tf_op jit(solution)/shard_map/all_gather | solution.py:124
  237.1 270.9 %copy-start.1 = (bf16[1024,128]{1,0:T(8,128)(2,1)S(1)}, bf16[1024,128]{1,0:T(8,128)(2,1)}, u32[]{:S(2)}) copy-start(bf16[1024,128]{1,0:T(8,128)(2,1)} %param.17) | copy-start | bytes 786436
  529.2 1.9 copy-start.2
  531.1 36.9 %copy-start.5 = (bf16[128,128]{1,0:T(8,128)(2,1)S(1)}, bf16[128,128]{1,0:T(8,128)(2,1)}, u32[]{:S(2)}) copy-start(bf16[128,128]{1,0:T(8,128)(2,1)} %param.19) | copy-start | bytes 98308
  543.1 25.3 %copy-start.3 = (bf16[128,128]{1,0:T(8,128)(2,1)S(1)}, bf16[128,128]{1,0:T(8,128)(2,1)}, u32[]{:S(2)}) copy-start(bf16[128,128]{1,0:T(8,128)(2,1)} %param.18) | copy-start | bytes 98308
  767.0 23.3 %copy-start.4 = (bf16[128,128]{1,0:T(8,128)(2,1)S(1)}, bf16[128,128]{1,0:T(8,128)(2,1)}, u32[]{:S(2)}) copy-start(bf16[128,128]{1,0:T(8,128)(2,1)} %param.23) | copy-start | bytes 98308
  767.0 23.4 %copy-start.6 = (bf16[128,128]{1,0:T(8,128)(2,1)S(1)}, bf16[128,128]{1,0:T(8,128)(2,1)}, u32[]{:S(2)}) copy-start(bf16[128,128]{1,0:T(8,128)(2,1)} %param.22) | copy-start | bytes 98308
  783.6 25.1 %all-to-all-start.5 = ((bf16[16,64,256]{2,0,1:T(8,128)(2,1)}), bf16[16,64,256]{2,0,1:T(8,128)(2,1)S(1)}, u32[]{:S(2)}, u32[]{:S(2)}) async-start(bf16[16,64,256]{2,0,1:T(8,128)(2,1)} %copy.78), calls=%async_computation.5 | async-start | bytes 1048576 | tf_op jit(solution)/shard_map/all_to_all | solution.py:126
Sparse Core Ops, SparseCore 0:
  10.8 224.3 all-gather.7
  237.4 218.1 all-gather.9
  457.9 50.1 all-reduce.1
  568.1 192.1 all-gather.5
where the time goes:
time: 819 us; the launch traced here: 817 us
  waiting for transfers between devices  653 us (80%)
  blocking collectives  85.8 us (10%)
  matrix products  29.9 us (4%)
  local copies, waits for them, and re-layouts  23.1 us (3%)
  between operations  13.5 us (2%)
    all_gather x1, waiting for transfers between devices, on_device(): lax.all_gather(left_proj, ('row', 'seq'), axis=0, tiled=True)  222 us
    all_gather x1, waiting for transfers between devices, on_device(): lax.all_gather(right_proj, ('row', 'seq'), axis=0, tiled=True)  218 us
    all_gather x1, waiting for transfers between devices, on_device(): lax.all_gather(right_local, 'row', axis=1, tiled=True)  154 us
    psum x1, waiting for transfers between devices, spread_2(): return lax.psum(jnp.where(mine, shard, jnp.zeros_like(shard)), axis)  40.3 us
    all_to_all x1, blocking collectives, on_device(): lax.all_to_all(lax.all_to_all(left_first, 'col', split_axis=0, concat_axi...  26.7 us
    all_to_all x1, blocking collectives, on_device(): lax.all_to_all(lax.all_to_all(right_first, 'col', split_axis=0, concat_ax...  24 us
    all_to_all x1, waiting for transfers between devices, on_device(): lax.all_to_all(lax.all_to_all(product, 'col', split_axis=2, concat_axis=0...  17.9 us
  transfers between devices with their start and end apart: 5, of which 5 were waited for; matrix products, arithmetic and copies ran while one was open for 2% of the time, Pallas kernels for 0%

commit v1 on v0

--- a/solution.py
+++ b/solution.py
@@ -4,6 +4,13 @@
 from jax.sharding import PartitionSpec as P
 
 EPS = 1e-05
+
+
+def exchange_gather(value, axis, dim):
+    n_dev = lax.axis_size(axis)
+    pieces = jnp.stack([value for _ in range(n_dev)])
+    pieces = lax.all_to_all(pieces, axis, split_axis=0, concat_axis=0)
+    return jnp.concatenate(pieces, axis=dim)
 
 
 def spread_2(shard, axis, root):
@@ -60,7 +67,7 @@
     index_row = lax.axis_index("row")
     root_col = index_row // per_col
     left_all, right_all = (
-        lax.all_gather(left_proj, ("row", "seq"), axis=0, tiled=True),
+        exchange_gather(left_proj, ("row", "seq"), 0),
         lax.all_gather(right_proj, ("row", "seq"), axis=0, tiled=True),
     )
     index_seq = lax.axis_index("seq")

time: 819 us -> 616 us (0.75)
  waiting for transfers between devices: 653 us -> 400 us
  starting transfers between devices: 6.87 us -> 24.2 us
  local copies, waits for them, and re-layouts: 23.1 us -> 38.7 us
  other arithmetic: 4.87 us -> 18.1 us
    all_gather x1 -> x0, waiting for transfers between devices: 222 us -> none  [on_device(): lax.all_gather(left_proj, ('row', 'seq'), axis=0, tiled=True)]
    all_to_all x0 -> x1, waiting for transfers between devices: none -> 51.6 us  [exchange_gather(): pieces = lax.all_to_all(pieces, axis, split_axis=0, concat_axis=0)]
    all_gather x1, waiting for transfers between devices: 218 us -> 178 us  [on_device(): lax.all_gather(right_proj, ('row', 'seq'), axis=0, tiled=True)]
    psum x1, waiting for transfers between devices: 40.3 us -> 0.03 us  [spread_2(): return lax.psum(jnp.where(mine, shard, jnp.zeros_like(shard)), axis)]
    all_to_all x0 -> x1, starting transfers between devices: none -> 17.4 us  [exchange_gather(): pieces = lax.all_to_all(pieces, axis, split_axis=0, concat_axis=0)]
    another operation x0 -> x1, other arithmetic: none -> 13.2 us  [exchange_gather(): pieces = jnp.stack([value for _ in range(n_dev)])]
    unnamed x19 -> x24, local copies, waits for them, and re-layouts: 3.2 us -> 12 us
  transfers between devices with their start and end apart: 5 -> 5, of which waited for: 5 -> 4; matrix products, arithmetic and copies ran while one was open for 2% -> 4% of each run, Pallas kernels for 0% -> 0%
where the time goes in v1:
time: 616 us; the launch traced here: 614 us
  waiting for transfers between devices  400 us (65%)
  blocking collectives  85.9 us (14%)
  local copies, waits for them, and re-layouts  38.7 us (6%)
  matrix products  31.2 us (5%)
  starting transfers between devices  24.2 us (4%)
  other arithmetic  18.1 us (3%)
  between operations  15.2 us (2%)
    all_gather x1, waiting for transfers between devices, on_device(): lax.all_gather(right_proj, ('row', 'seq'), axis=0, tiled=True)  178 us
    all_gather x1, waiting for transfers between devices, on_device(): lax.all_gather(right_local, 'row', axis=1, tiled=True)  154 us
    all_to_all x1, waiting for transfers between devices, exchange_gather(): pieces = lax.all_to_all(pieces, axis, split_axis=0, concat_axis=0)  51.6 us
    all_to_all x1, blocking collectives, on_device(): lax.all_to_all(lax.all_to_all(left_first, 'col', split_axis=0, concat_axi...  25.9 us
    all_to_all x1, blocking collectives, on_device(): lax.all_to_all(lax.all_to_all(right_first, 'col', split_axis=0, concat_ax...  21.5 us
    all_to_all x1, starting transfers between devices, exchange_gather(): pieces = lax.all_to_all(pieces, axis, split_axis=0, concat_axis=0)  17.4 us
    all_to_all x1, waiting for transfers between devices, on_device(): lax.all_to_all(lax.all_to_all(product, 'col', split_axis=2, concat_axis=0...  16.9 us
    all_to_all x1, blocking collectives, on_device(): lax.all_to_all(right_first, 'col', split_axis=0, concat_axis=2, tiled=True)  13.4 us
  transfers between devices with their start and end apart: 5, of which 4 were waited for; matrix products, arithmetic and copies ran while one was open for 4% of the time, Pallas kernels for 0%

profile of v1, /device:TPU:8, one launch (start us, length us, event | category | flops | bytes accessed | tf_op | source)
XLA Modules:
  0.0 613.9 jit_solution(3190073703241617097)
XLA Ops:
  10.9 6.1 stack.3
  17.5 13.2 %reduce.4 = bf16[128,8192]{1,0:T(8,128)(2,1)S(1)} reduce(bf16[128,1,8192]{2,1,0:T(2,128)(2,1)} %stack.3, bf16[]{:T(256)} %broadcast.99), dimensions={1}, to_apply=%stack.3.reduce_sub_computation | reduce | bytes 4194306 | tf_op jit(solution)/shard_map/stack | solution.py:11
  30.8 2.8 reshape.112
  33.6 17.4 %all-to-all-start = ((bf16[128,2,4096]{2,1,0:T(2,128)(2,1)}), bf16[128,2,4096]{2,1,0:T(2,128)(2,1)S(1)}, u32[]{:S(2)}, u32[]{:S(2)}) async-start(bf16[128,2,4096]{2,1,0:T(2,128)(2,1)} %reshape.112), calls=%async_computation | async-start | bytes 4194304 | tf_op jit(solution)/shard_map/all_to_all | solution.py:12
  52.2 51.6 %all-to-all-done = bf16[128,2,4096]{2,1,0:T(2,128)(2,1)S(1)} async-done(((bf16[128,2,4096]{2,1,0:T(2,128)(2,1)}), bf16[128,2,4096]{2,1,0:T(2,128)(2,1)S(1)}, u32[]{:S(2)}, u32[]{:S(2)}) %all-to-all-start) | async-done | bytes 2097184 | tf_op jit(solution)/shard_map/all_to_all | solution.py:12
  103.8 6.8 %reshape.113 = bf16[128,1,8192]{2,1,0:T(2,128)(2,1)} reshape(bf16[128,2,4096]{2,1,0:T(2,128)(2,1)S(1)} %all-to-all-done) | data formatting | bytes 4194304
  112.5 178.0 %all-gather.6.cloned.1.call-done = bf16[128,1,8192]{2,1,0:T(2,128)(2,1)} async-done(((bf16[1,1,8192]{2,1,0:T(2,128)(2,1)}), bf16[128,1,8192]{2,1,0:T(2,128)(2,1)}) %all-gather.6.cloned.1.call-update) | async-done | bytes 2097168 | tf_op jit(solution)/shard_map/all_gather | solution.py:71
  290.5 9.1 %copy.50 = bf16[128,1,8192]{0,2,1:T(8,128)(2,1)} copy(bf16[128,1,8192]{2,1,0:T(2,128)(2,1)} %all-gather.6.cloned.1.call-done) | data formatting | bytes 4194304 | tf_op jit(solution)/shard_map/all_gather | solution.py:71
  299.6 3.0 copy.51
  302.7 21.2 %while.10 = (s32[]{:T(128)}, bf16[8,256,128]{2,1,0:T(8,128)(2,1)S(1)}, bf16[8,256,128]{2,1,0:T(8,128)(2,1)}, bf16[8,128,32]{1,2,0:T(8,128)(2,1)}, bf16[128,256,3...) while((s32[]{:T(128)}, bf16[8,256,128]{2,1,0:T(8,128)(2,1)S(1)}, ...), condition=%wide.region_4.5_spmd, body=%wide.region_3.4_spmd.sunk | while | flops 134840320 | bytes 4596305 | solution.py:96
  306.7 1.2 fusion.68
  312.0 1.2 fusion.68
  317.3 1.2 fusion.68
  326.5 13.4 %all_to_all.104 = bf16[128,8,256]{2,1,0:T(8,128)(2,1)S(1)} all-to-all(bf16[128,8,256]{2,1,0:T(8,128)(2,1)S(1)} %copy.55), channel_id=1, replica_groups=mesh['row'=16,'col'=4,'seq'=8] {'col'}, dimensions={0} | all-to-all | bytes 1048576 | tf_op jit(solution)/shard_map/all_to_all | solution.py:124
  340.0 21.5 %all_to_all.105 = bf16[32,8,1024]{2,1,0:T(8,128)(2,1)S(1)} all-to-all(bf16[32,8,1024]{2,1,0:T(8,128)(2,1)S(1)} %bitcast.131), channel_id=1, replica_groups=mesh['row'=16,'col'=4,'seq'=8] {'seq'}, dimensions={0} | all-to-all | bytes 1048576 | tf_op jit(solution)/shard_map/all_to_all | solution.py:123
  363.5 11.8 %all_to_all.106 = bf16[128,8,256]{2,1,0:T(8,128)(2,1)S(1)} all-to-all(bf16[128,8,256]{2,1,0:T(8,128)(2,1)S(1)} %copy.52), channel_id=1, replica_groups=mesh['row'=16,'col'=4,'seq'=8] {'col'}, dimensions={0} | all-to-all | bytes 1048576 | tf_op jit(solution)/shard_map/all_to_all | solution.py:117
  375.3 25.9 %all_to_all.107 = bf16[32,8,1024]{2,1,0:T(8,128)(2,1)S(1)} all-to-all(bf16[32,8,1024]{2,1,0:T(8,128)(2,1)S(1)} %bitcast.134), channel_id=1, replica_groups=mesh['row'=16,'col'=4,'seq'=8] {'seq'}, dimensions={0} | all-to-all | bytes 1048576 | tf_op jit(solution)/shard_map/all_to_all | solution.py:116
  401.2 153.9 %all-gather.4.cloned.1.call-done = bf16[4,1024,1024]{2,1,0:T(8,128)(2,1)} async-done(((bf16[4,64,1024]{2,1,0:T(8,128)(2,1)}), bf16[4,1024,1024]{2,1,0:T(8,128)(2,1)}) %all-gather.4.cloned.1.call-update) | async-done | bytes 8388624 | tf_op jit(solution)/shard_map/all_gather | solution.py:131
  555.1 6.0 convolution_convert_fusion
  562.7 13.3 %all_to_all.108 = bf16[4,2,32768]{2,1,0:T(2,128)(2,1)S(1)} all-to-all(bf16[4,2,32768]{2,1,0:T(2,128)(2,1)S(1)} %reshape.114), channel_id=1, replica_groups=mesh['row'=16,'col'=4,'seq'=8] {'col'}, dimensions={0} | all-to-all | bytes 1048576 | tf_op jit(solution)/shard_map/all_to_all | solution.py:134
  578.4 6.7 %all-to-all-start.6 = ((bf16[16,64,256]{2,0,1:T(8,128)(2,1)}), bf16[16,64,256]{2,0,1:T(8,128)(2,1)S(1)}, u32[]{:S(2)}, u32[]{:S(2)}) async-start(bf16[16,64,256]{2,0,1:T(8,128)(2,1)} %copy.61), calls=%async_computation.6 | async-start | bytes 1048576 | tf_op jit(solution)/shard_map/all_to_all | solution.py:133
  585.1 1.4 fusion.16
  586.5 16.9 %all-to-all-done.6 = bf16[16,64,256]{2,0,1:T(8,128)(2,1)S(1)} async-done(((bf16[16,64,256]{2,0,1:T(8,128)(2,1)}), bf16[16,64,256]{2,0,1:T(8,128)(2,1)S(1)}, u32[]{:S(2)}, u32[]{:S(2)}) %all-to-all-start.6) | async-done | bytes 524320 | tf_op jit(solution)/shard_map/all_to_all | solution.py:133
  604.1 2.4 fusion.19
  (87 shorter events, 33.7 us)
Async XLA Ops:
  7.4 318.0 %copy-start = (bf16[128,128]{1,0:T(8,128)(2,1)S(1)}, bf16[128,128]{1,0:T(8,128)(2,1)}, u32[]{:S(2)}) copy-start(bf16[128,128]{1,0:T(8,128)(2,1)} %param.21) | copy-start | bytes 98308
  30.8 20.2 %copy-start.2 = (bf16[1,256,256]{2,1,0:T(8,128)(2,1)S(1)}, bf16[1,256,256]{2,1,0:T(8,128)(2,1)}, u32[]{:S(2)}) copy-start(bf16[1,256,256]{2,1,0:T(8,128)(2,1)} %param.14) | copy-start | bytes 393220
  30.8 20.2 %copy-start.8 = (bf16[256,32]{0,1:T(8,128)(2,1)S(1)}, bf16[256,32]{0,1:T(8,128)(2,1)}, u32[]{:S(2)}) copy-start(bf16[256,32]{0,1:T(8,128)(2,1)} %param.16) | copy-start | bytes 49156
  33.6 70.2 %all-to-all-start = ((bf16[128,2,4096]{2,1,0:T(2,128)(2,1)}), bf16[128,2,4096]{2,1,0:T(2,128)(2,1)S(1)}, u32[]{:S(2)}, u32[]{:S(2)}) async-start(bf16[128,2,4096]{2,1,0:T(2,128)(2,1)} %reshape.112), calls=%async_computation | async-start | bytes 4194304 | tf_op jit(solution)/shard_map/all_to_all | solution.py:12
  51.0 239.5 %all-gather.6.cloned.1.call-start = ((), (), s32[]{:S(2)}) async-start(), calls=%async_computation.9 | async-start | bytes 4227072 | tf_op jit(solution)/shard_map/all_gather | solution.py:71
  52.2 250.5 %all-reduce.2.cloned.1.call-start = ((), (), s32[]{:S(2)}) async-start(), calls=%async_computation.7 | async-start | bytes 131072 | tf_op jit(solution)/shard_map/psum | solution.py:18
  112.5 442.6 %all-gather.4.cloned.1.call-start = ((), (), s32[]{:S(2)}) async-start(), calls=%async_computation.8 | async-start | bytes 8912896 | tf_op jit(solution)/shard_map/all_gather | solution.py:131
  112.5 190.1 %copy-start.1 = (bf16[1024,128]{1,0:T(8,128)(2,1)S(1)}, bf16[1024,128]{1,0:T(8,128)(2,1)}, u32[]{:S(2)}) copy-start(bf16[1024,128]{1,0:T(8,128)(2,1)} %param.17) | copy-start | bytes 786436
  323.8 2.0 copy-start.3
  325.8 36.5 %copy-start.6 = (bf16[128,128]{1,0:T(8,128)(2,1)S(1)}, bf16[128,128]{1,0:T(8,128)(2,1)}, u32[]{:S(2)}) copy-start(bf16[128,128]{1,0:T(8,128)(2,1)} %param.19) | copy-start | bytes 98308
  339.9 22.9 %copy-start.4 = (bf16[128,128]{1,0:T(8,128)(2,1)S(1)}, bf16[128,128]{1,0:T(8,128)(2,1)}, u32[]{:S(2)}) copy-start(bf16[128,128]{1,0:T(8,128)(2,1)} %param.18) | copy-start | bytes 98308
  561.8 23.3 %copy-start.5 = (bf16[128,128]{1,0:T(8,128)(2,1)S(1)}, bf16[128,128]{1,0:T(8,128)(2,1)}, u32[]{:S(2)}) copy-start(bf16[128,128]{1,0:T(8,128)(2,1)} %param.23) | copy-start | bytes 98308
  561.8 23.3 %copy-start.7 = (bf16[128,128]{1,0:T(8,128)(2,1)S(1)}, bf16[128,128]{1,0:T(8,128)(2,1)}, u32[]{:S(2)}) copy-start(bf16[128,128]{1,0:T(8,128)(2,1)} %param.22) | copy-start | bytes 98308
  578.4 25.1 %all-to-all-start.6 = ((bf16[16,64,256]{2,0,1:T(8,128)(2,1)}), bf16[16,64,256]{2,0,1:T(8,128)(2,1)S(1)}, u32[]{:S(2)}, u32[]{:S(2)}) async-start(bf16[16,64,256]{2,0,1:T(8,128)(2,1)} %copy.61), calls=%async_computation.6 | async-start | bytes 1048576 | tf_op jit(solution)/shard_map/all_to_all | solution.py:133
Sparse Core Ops, SparseCore 0:
  53.9 236.4 all-gather.5
Sparse Core Ops, SparseCore 1:
  112.5 47.5 all-reduce.1
  362.4 192.6 all-gather.3
